TPU v7x, 32 devices: a whole 2x2x4 slice. The times are simulated.
32 devices in a mesh: dp: 2 (over x), ctx: 4 (over z), tp: 4 (over y, core).
Axes of the slice: x: 2, y: 2, z: 4, core: 2. Of those that a mesh axis runs over, the one named last changes fastest.
Arguments:
- hidden_in: bfloat16 [2, 2, 2048, 768], P(None, 'dp', 'ctx'), may hold values from -6 to 6
- prefix: int32 [2, 2], P(None, 'dp'), may hold values from 204 to 1024
- block_order: int32 [8], replicated, may hold values from 0 to 7, each once
- qkv_weight: bfloat16 [3, 768, 768], P(None, 'dp', 'tp'), may hold values from -0.3125 to 0.3125
- out_weight: bfloat16 [768, 768], P('tp', 'dp'), may hold values from -2.5 to 2.5
- up_weight: bfloat16 [768, 3072], P('dp', 'tp'), may hold values from -0.21875 to 0.21875
- down_weight: bfloat16 [3072, 768], P('tp', 'dp'), may hold values from -0.4375 to 0.4375
- ln_gains: bfloat16 [2, 768], P(None, 'dp'), may hold values from 0.5 to 1.5
- ln_shifts: bfloat16 [2, 768], P(None, 'dp'), may hold values from -2 to 2
- cotangent: bfloat16 [2, 2, 2048, 768], P(None, 'dp', 'ctx'), may hold values from -6 to 6
Outputs:
- block_out: bfloat16 [2, 2, 2048, 768], P(None, 'dp', 'ctx')
- grad_in: float32 [2, 2, 2048, 768], P(None, 'dp', 'ctx')
- grad_qkv: float32 [3, 768, 768], P(None, 'dp', 'tp')
- grad_out: float32 [768, 768], P('tp', 'dp')
- grad_up: float32 [768, 3072], P('dp', 'tp')
- grad_down: float32 [3072, 768], P('tp', 'dp')
- grad_gains: float32 [2, 768], P(None, 'dp')
- grad_shifts: float32 [2, 768], P(None, 'dp')
Inputs may be any that keep to these rules, and one draw needn't show every extreme that they name: `prefix`: leading positions of each sequence that all of its queries see. `block_order`: each of the 2 * 4 block numbers appears once.
All inputs are finite; a program needn't handle non-finite values.
Results may differ from a plain program's by a relative error of at most 0.012.
The roundings to bfloat16 on the way count: a program that leaves them out, or rounds other values in their place, can miss the bound.
Values may be sent and summed in bfloat16 or wider, within the bound.
A program may use at most 128 MiB of HBM per device.

v0:
```python
import jax
import jax.numpy as jnp
from jax import lax
from jax.sharding import PartitionSpec as P

HEAD_DIM = 64
DEPTH = 12
EPS = 1e-05
GELU_C = 0.7978845608028654
GELU_A = 0.044715
NEG = -1e30
ROW_BLOCK = 512


def apply_layer_norm(values, norm_gain, norm_shift):
    row_mean = jnp.mean(values, axis=1, keepdims=True)
    centered_input = values - row_mean
    inverse_deviation = lax.rsqrt(
        jnp.mean(centered_input * centered_input, axis=1, keepdims=True) + EPS
    )
    normalized_input = centered_input * inverse_deviation
    return (normalized_input * norm_gain + norm_shift, normalized_input, inverse_deviation)


def norm_backward(normed_gradient, normalized_input, inverse_deviation, norm_gain):
    scaled_gradient = normed_gradient * norm_gain
    return inverse_deviation * (
        scaled_gradient
        - jnp.mean(scaled_gradient, axis=1, keepdims=True)
        - normalized_input * jnp.mean(scaled_gradient * normalized_input, axis=1, keepdims=True)
    )


def gelu_value(u):
    return 0.5 * u * (1.0 + jnp.tanh(GELU_C * (u + GELU_A * u * u * u)))


def gelu_slope(u):
    inner = jnp.tanh(GELU_C * (u + GELU_A * u * u * u))
    return 0.5 * (1.0 + inner) + 0.5 * u * (1.0 - inner * inner) * GELU_C * (
        1.0 + 3.0 * GELU_A * u * u
    )


def block_positions(block_order, rows, half):
    slots = jnp.arange(block_order.shape[0], dtype=jnp.int32)
    picked = jnp.where((rows // half)[:, None] == slots[None, :], block_order[None, :], 0)
    return jnp.sum(picked, axis=1) * half + rows % half


def fetch_weights(qkv_weight, out_weight, up_weight, down_weight, ln_gains, ln_shifts):
    return (
        lax.all_gather(qkv_weight, "dp", axis=1, tiled=True),
        lax.all_gather(out_weight, "dp", axis=1, tiled=True),
        lax.all_gather(up_weight, "dp", axis=0, tiled=True),
        lax.all_gather(down_weight, "dp", axis=1, tiled=True),
        lax.all_gather(ln_gains, "dp", axis=1, tiled=True),
        lax.all_gather(ln_shifts, "dp", axis=1, tiled=True),
    )


def body(
    hidden_in,
    prefix,
    block_order,
    qkv_weight,
    out_weight,
    up_weight,
    down_weight,
    ln_gains,
    ln_shifts,
    cotangent,
):
    micro = hidden_in.shape[0]
    tokens = hidden_in.shape[2]
    width = hidden_in.shape[3]
    local_width = qkv_weight.shape[2]
    head_dim = HEAD_DIM
    local_heads = local_width // head_dim
    seq_len = tokens * lax.axis_size("ctx")
    half = tokens // 2
    branch = DEPTH ** (-0.5)
    scale = head_dim ** (-0.5)
    block_rows = min(tokens, ROW_BLOCK)
    blocks = tokens // block_rows
    query_rows = lax.axis_index("ctx") * tokens + jnp.arange(tokens, dtype=jnp.int32)
    key_rows = jnp.arange(seq_len, dtype=jnp.int32)
    query_pos = block_positions(block_order, query_rows, half)
    key_pos = block_positions(block_order, key_rows, half)
    acc_qkv = jnp.zeros((3, width, local_width), jnp.float32)
    acc_out = jnp.zeros((local_width, width), jnp.float32)
    acc_up = jnp.zeros((width, up_weight.shape[1]), jnp.float32)
    acc_down = jnp.zeros((down_weight.shape[0], width), jnp.float32)
    acc_gains = jnp.zeros((2, width), jnp.float32)
    acc_shifts = jnp.zeros((2, width), jnp.float32)
    results = []
    input_gradient_list = []
    for index in range(micro):
        full = fetch_weights(qkv_weight, out_weight, up_weight, down_weight, ln_gains, ln_shifts)
        qkv_full, out_full, up_full, down_full, gains_full, shifts_full = full
        norm_gains = gains_full.astype(jnp.float32)
        norm_shifts = shifts_full.astype(jnp.float32)
        input_rows = hidden_in[index, 0].astype(jnp.float32)
        allowed = (key_pos[None, :] <= query_pos[:, None]) | (key_pos[None, :] < prefix[index, 0])
        first_normed, normalized_first1, inverse_deviation1 = apply_layer_norm(
            input_rows, norm_gains[0], norm_shifts[0]
        )
        h1 = first_normed.astype(jnp.bfloat16)
        qkv = jnp.einsum("td,kde->kte", h1, qkv_full, preferred_element_type=jnp.float32).astype(
            jnp.bfloat16
        )
        keys_flat, values_flat = (
            lax.all_gather(qkv[1], "ctx", axis=0, tiled=True),
            lax.all_gather(qkv[2], "ctx", axis=0, tiled=True),
        )
        keys = keys_flat.reshape(seq_len, local_heads, head_dim)
        values = values_flat.reshape(seq_len, local_heads, head_dim)
        q_blocks = qkv[0].reshape(blocks, block_rows, local_heads, head_dim)
        a_blocks = allowed.reshape(blocks, block_rows, seq_len)

        def attend(item):
            q_blk, allow_blk = item
            scores = (
                jnp.einsum("qhd,khd->hqk", q_blk, keys, preferred_element_type=jnp.float32) * scale
            )
            scores = jnp.where(allow_blk[None], scores, NEG)
            top = jnp.max(scores, axis=2, keepdims=True)
            expd = jnp.exp(scores - top)
            total = jnp.sum(expd, axis=2, keepdims=True)
            prob = (expd / total).astype(jnp.bfloat16)
            mixed = jnp.einsum("hqk,khd->qhd", prob, values, preferred_element_type=jnp.float32)
            return (mixed.astype(jnp.bfloat16), (top + jnp.log(total))[:, :, 0])

        heads_out, logsum = lax.map(attend, (q_blocks, a_blocks))
        heads = heads_out.reshape(tokens, local_width)
        attn_part = jnp.dot(heads, out_full, preferred_element_type=jnp.float32)
        attn = lax.psum(attn_part, "tp")
        middle_state = input_rows + branch * attn
        second_normed, normalized_second2, inverse_deviation2 = apply_layer_norm(
            middle_state, norm_gains[1], norm_shifts[1]
        )
        h2 = second_normed.astype(jnp.bfloat16)
        up = jnp.dot(h2, up_full, preferred_element_type=jnp.float32)
        act = gelu_value(up).astype(jnp.bfloat16)
        mlp_part = jnp.dot(act, down_full, preferred_element_type=jnp.float32)
        mlp = lax.psum(mlp_part, "tp")
        results.append((middle_state + branch * mlp).astype(jnp.bfloat16))
        qkv_full, out_full, up_full, down_full, gains_full, shifts_full = fetch_weights(
            qkv_weight, out_weight, up_weight, down_weight, ln_gains, ln_shifts
        )
        upstream_gradient = cotangent[index, 0].astype(jnp.float32)
        d_mlp = (branch * upstream_gradient).astype(jnp.bfloat16)
        grad_down = jnp.einsum("tf,td->fd", act, d_mlp, preferred_element_type=jnp.float32)
        d_act = jnp.einsum("td,fd->tf", d_mlp, down_full, preferred_element_type=jnp.float32)
        d_up = (d_act * gelu_slope(up)).astype(jnp.bfloat16)
        grad_up = jnp.einsum("td,tf->df", h2, d_up, preferred_element_type=jnp.float32)
        n2_back = jnp.einsum("tf,df->td", d_up, up_full, preferred_element_type=jnp.float32)
        second_norm_gradient = lax.psum(n2_back, "tp")
        middle_gradient = upstream_gradient + norm_backward(
            second_norm_gradient, normalized_second2, inverse_deviation2, norm_gains[1]
        )
        d_attn = (branch * middle_gradient).astype(jnp.bfloat16)
        grad_out = jnp.einsum("te,td->ed", heads, d_attn, preferred_element_type=jnp.float32)
        d_heads = jnp.einsum(
            "td,ed->te", d_attn, out_full, preferred_element_type=jnp.float32
        ).astype(jnp.bfloat16)
        dh_blocks = d_heads.reshape(blocks, block_rows, local_heads, head_dim)

        def attend_back(carry, item):
            key_sum, value_sum = carry
            q_blk, allow_blk, lse_blk, dh_blk = item
            scores = (
                jnp.einsum("qhd,khd->hqk", q_blk, keys, preferred_element_type=jnp.float32) * scale
            )
            scores = jnp.where(allow_blk[None], scores, NEG)
            prob = jnp.exp(scores - lse_blk[:, :, None])
            prob_low = prob.astype(jnp.bfloat16)
            d_prob = jnp.einsum("qhd,khd->hqk", dh_blk, values, preferred_element_type=jnp.float32)
            d_scores = (prob * (d_prob - jnp.sum(prob * d_prob, axis=2, keepdims=True))).astype(
                jnp.bfloat16
            )
            d_query = (
                jnp.einsum("hqk,khd->qhd", d_scores, keys, preferred_element_type=jnp.float32)
                * scale
            ).astype(jnp.bfloat16)
            key_sum = (
                key_sum
                + jnp.einsum("hqk,qhd->khd", d_scores, q_blk, preferred_element_type=jnp.float32)
                * scale
            )
            value_sum = value_sum + jnp.einsum(
                "hqk,qhd->khd", prob_low, dh_blk, preferred_element_type=jnp.float32
            )
            return ((key_sum, value_sum), d_query)

        zero_kv = jnp.zeros((seq_len, local_heads, head_dim), jnp.float32)
        (key_sum, value_sum), d_query = lax.scan(
            attend_back, (zero_kv, zero_kv), (q_blocks, a_blocks, logsum, dh_blocks)
        )
        d_keys, d_values = (
            lax.psum_scatter(
                key_sum.reshape(seq_len, local_width), "ctx", scatter_dimension=0, tiled=True
            ),
            lax.psum_scatter(
                value_sum.reshape(seq_len, local_width), "ctx", scatter_dimension=0, tiled=True
            ),
        )
        d_qkv = jnp.stack(
            [
                d_query.reshape(tokens, local_width),
                d_keys.astype(jnp.bfloat16),
                d_values.astype(jnp.bfloat16),
            ]
        )
        grad_qkv = jnp.einsum("td,kte->kde", h1, d_qkv, preferred_element_type=jnp.float32)
        n1_back = jnp.einsum("kte,kde->td", d_qkv, qkv_full, preferred_element_type=jnp.float32)
        first_norm_gradient = lax.psum(n1_back, "tp")
        input_gradient_list.append(
            middle_gradient
            + norm_backward(
                first_norm_gradient, normalized_first1, inverse_deviation1, norm_gains[0]
            )
        )
        acc_gains = acc_gains + jnp.stack(
            [
                jnp.sum(first_norm_gradient * normalized_first1, axis=0),
                jnp.sum(second_norm_gradient * normalized_second2, axis=0),
            ]
        )
        acc_shifts = acc_shifts + jnp.stack(
            [jnp.sum(first_norm_gradient, axis=0), jnp.sum(second_norm_gradient, axis=0)]
        )
        acc_qkv = acc_qkv + grad_qkv
        acc_out = acc_out + grad_out
        acc_up = acc_up + grad_up
        acc_down = acc_down + grad_down
    whole_qkv, whole_out, whole_up, whole_down, whole_gains, whole_shifts = lax.psum(
        (acc_qkv, acc_out, acc_up, acc_down, acc_gains, acc_shifts), "ctx"
    )
    owned = (
        lax.psum_scatter(whole_qkv, "dp", scatter_dimension=1, tiled=True),
        lax.psum_scatter(whole_out, "dp", scatter_dimension=1, tiled=True),
        lax.psum_scatter(whole_up, "dp", scatter_dimension=0, tiled=True),
        lax.psum_scatter(whole_down, "dp", scatter_dimension=1, tiled=True),
        lax.psum_scatter(whole_gains, "dp", scatter_dimension=1, tiled=True),
        lax.psum_scatter(whole_shifts, "dp", scatter_dimension=1, tiled=True),
    )
    block_out = jnp.stack(results)[:, None]
    grad_in = jnp.stack(input_gradient_list)[:, None]
    return (block_out, grad_in, owned[0], owned[1], owned[2], owned[3], owned[4], owned[5])


def solution(mesh):
    in_specs = (
        P(None, "dp", "ctx", None),
        P(None, "dp"),
        P(),
        P(None, "dp", "tp"),
        P("tp", "dp"),
        P("dp", "tp"),
        P("tp", "dp"),
        P(None, "dp"),
        P(None, "dp"),
        P(None, "dp", "ctx", None),
    )
    out_specs = (
        P(None, "dp", "ctx", None),
        P(None, "dp", "ctx", None),
        P(None, "dp", "tp"),
        P("tp", "dp"),
        P("dp", "tp"),
        P("tp", "dp"),
        P(None, "dp"),
        P(None, "dp"),
    )
    return jax.shard_map(body, mesh=mesh, in_specs=in_specs, out_specs=out_specs, check_vma=False)
```

profile of v0, /device:TPU:0, one launch (start us, length us, event | category | flops | bytes accessed | tf_op | source)
XLA Modules:
  0.0 766.6 jit_solution(9417610063547408217)
XLA Ops:
  10.2 5.5 all_gather.20
  15.7 4.5 all_gather.21
  22.8 5.9 all_gather.49
  28.7 9.4 %all_gather.22 = bf16[3,768,192]{1,2,0:T(8,128)(2,1)S(1)} all-gather(bf16[3,384,192]{1,2,0:T(8,128)(2,1)S(1)} %copy-done.43), channel_id=1, replica_groups=mesh['dp'=2,'ctx'=4,'tp'=4] {'dp'}, dimensions={1}, use_global_device_ids=true | all-gather | bytes 1327104 | tf_op jit(solution)/shard_map/all_gather | solution.py:53
  39.8 19.5 %all-gather.3 = bf16[1,2048,192]{1,2,0:T(8,128)(2,1)S(1)} all-gather(bf16[1,512,192]{1,2,0:T(8,128)(2,1)S(1)} %get-tuple-element.187), channel_id=5, replica_groups=mesh['dp'=2,'ctx'=4,'tp'=4] {'ctx'}, dimensions={1}, use_global_device_ids=true | all-gather | bytes 983040 | tf_op jit(solution)/shard_map/all_gather | solution.py:113
  59.3 17.9 %all-gather.2 = bf16[1,2048,192]{1,2,0:T(8,128)(2,1)S(1)} all-gather(bf16[1,512,192]{1,2,0:T(8,128)(2,1)S(1)} %get-tuple-element.189), channel_id=4, replica_groups=mesh['dp'=2,'ctx'=4,'tp'=4] {'ctx'}, dimensions={1}, use_global_device_ids=true | all-gather | bytes 983040 | tf_op jit(solution)/shard_map/all_gather | solution.py:114
  78.2 17.1 %all-gather.1 = bf16[1,2048,192]{1,2,0:T(8,128)(2,1)S(1)} all-gather(bf16[1,512,192]{1,2,0:T(8,128)(2,1)S(1)} %get-tuple-element.184), channel_id=3, replica_groups=mesh['dp'=2,'ctx'=4,'tp'=4] {'ctx'}, dimensions={1}, use_global_device_ids=true | all-gather | bytes 983040 | tf_op jit(solution)/shard_map/all_gather | solution.py:113
  95.3 15.7 %all-gather = bf16[1,2048,192]{1,2,0:T(8,128)(2,1)S(1)} all-gather(bf16[1,512,192]{1,2,0:T(8,128)(2,1)S(1)} %get-tuple-element.186), channel_id=2, replica_groups=mesh['dp'=2,'ctx'=4,'tp'=4] {'ctx'}, dimensions={1}, use_global_device_ids=true | all-gather | bytes 983040 | tf_op jit(solution)/shard_map/all_gather | solution.py:114
  114.5 2.7 fusion.124
  119.1 2.6 copy-done
  121.7 3.6 fusion.65
  126.9 2.7 fusion.123
  131.5 2.6 copy-done.1
  134.1 3.1 fusion.64
  140.2 68.0 %all-reduce.14.cloned.1.call-done = (f32[512,768]{1,0:T(8,128)}, f32[512,768]{1,0:T(8,128)}) async-done(((f32[512,768]{1,0:T(8,128)}, f32[512,768]{1,0:T(8,128)}), (f32[512,768]{1,0:T(8,128)}, f32[512,768]{1,0:T(8,128)})) %all-reduce.14.cloned.1.call-update) | async-done | bytes 3145744 | tf_op jit(solution)/shard_map/psum | solution.py:137
  208.2 2.4 fusion.116
  211.8 3.9 fusion.114
  217.8 3.6 fusion.56
  227.0 68.7 %all-reduce.12.cloned.1.call-done = (f32[512,768]{1,0:T(8,128)}, f32[512,768]{1,0:T(8,128)}) async-done(((f32[512,768]{1,0:T(8,128)}, f32[512,768]{1,0:T(8,128)}), (f32[512,768]{1,0:T(8,128)}, f32[512,768]{1,0:T(8,128)})) %all-reduce.12.cloned.1.call-update) | async-done | bytes 3145744 | tf_op jit(solution)/shard_map/psum | solution.py:158
  295.7 3.8 multiply_reduce_fusion.3
  303.7 7.9 %fusion.6 = f32[3,64,2048]{2,1,0:T(8,128)} fusion(bf16[512,3,64]{0,2,1:T(8,128)(2,1)S(1)} %bitcast.237, f32[3,512,2048]{2,1,0:T(8,128)} %copy-done, f32[3,512]{1,0:T(4,128)S(1)} %log_add_fusion.1), kind=kOutput, calls=%fused_computation.17 | convolution fusion | flops 408944640 | bytes 14358528 | tf_op jit(solution)/shard_map/while/body/eval_jaxpr/hqk,qhd->khd/dot_general | solution.py:191
  313.8 8.2 %fusion.4 = f32[3,64,2048]{2,1,0:T(8,128)} fusion(bf16[512,3,64]{0,2,1:T(8,128)(2,1)S(1)} %bitcast.239, f32[3,512,2048]{2,1,0:T(8,128)} %copy-done.1, f32[3,512]{1,0:T(4,128)S(1)} %log_add_fusion), kind=kOutput, calls=%fused_computation.16 | convolution fusion | flops 408944640 | bytes 14358528 | tf_op jit(solution)/shard_map/while/body/eval_jaxpr/hqk,qhd->khd/dot_general | solution.py:191
  322.9 6.6 multiply_reduce_fusion
  329.5 6.5 multiply_convert_fusion
  336.0 2.9 convolution_multiply_fusion
  339.9 6.6 multiply_reduce_fusion.1
  346.6 6.4 multiply_convert_fusion.1
  353.0 2.9 convolution_multiply_fusion.1
  356.6 4.1 fusion.112
  360.7 3.9 fusion.111
  364.6 5.6 fusion.63
  370.2 2.7 fusion.62
  374.0 10.4 %reduce-scatter.21.cloned.1.call-done = f32[512,192]{0,1:T(8,128)} async-done(((f32[2048,192]{0,1:T(8,128)}), f32[512,192]{0,1:T(8,128)}) %reduce-scatter.21.cloned.1.call-update) | async-done | bytes 393232 | tf_op jit(solution)/shard_map/reduce_scatter | solution.py:204
  385.4 35.6 %reduce-scatter.19.cloned.1.call-done = f32[512,192]{0,1:T(8,128)} async-done(((f32[2048,192]{0,1:T(8,128)}), f32[512,192]{0,1:T(8,128)}) %reduce-scatter.19.cloned.1.call-update) | async-done | bytes 393232 | tf_op jit(solution)/shard_map/reduce_scatter | solution.py:201
  422.7 3.2 convolution_bitcast_fusion
  426.0 31.6 %reduce-scatter.15.cloned.1.call-done = f32[512,192]{0,1:T(8,128)} async-done(((f32[2048,192]{0,1:T(8,128)}), f32[512,192]{0,1:T(8,128)}) %reduce-scatter.15.cloned.1.call-update) | async-done | bytes 393232 | tf_op jit(solution)/shard_map/reduce_scatter | solution.py:201
  459.3 3.3 convolution_bitcast_fusion.1
  466.7 3.1 fusion.113
  469.8 2.5 convolution_add_fusion.1
  472.4 2.9 fusion.73
  475.3 2.6 convolution_add_fusion
  483.8 97.4 %all-reduce.10.cloned.1.call-done = (f32[512,768]{1,0:T(8,128)}, f32[512,768]{1,0:T(8,128)}, f32[512,768]{1,0:T(8,128)}, f32[512,768]{1,0:T(8,128)}) async-done(((f32[512,768]{1,0:T(8,128)}, f32[512,768]{1,0:T(8,128)}, f32[512,768]{1,0:T(8,128)}, f32[512,768]{1,0:T(8,128)}), (f32[512,768]{1,0:T(8,128)}, f32[512,768]{1,0:T(8,128)}, f32[512,768]{1,0:T(8,128)}, ...) | async-done | bytes 6291472 | tf_op jit(solution)/shard_map/psum | solution.py:146
  581.2 2.9 fusion.44
  595.7 5.8 reduce-scatter.33.cloned.1.call-done
  602.5 15.0 %reduce-scatter.31.cloned.1.call-done = f32[384,2]{1,0:T(8,128)} async-done(((f32[768,2]{1,0:T(8,128)}), f32[384,2]{1,0:T(8,128)}) %reduce-scatter.31.cloned.1.call-update) | async-done | bytes 3088
  618.5 12.6 %all-reduce.3 = (f32[2,384]{1,0:T(2,128)}, f32[2,384]{1,0:T(2,128)}) all-reduce(f32[2,384]{1,0:T(2,128)S(1)} %copy.25, f32[2,384]{1,0:T(2,128)S(1)} %copy.27), channel_id=1, replica_groups=mesh['dp'=2,'ctx'=4,'tp'=4] {'ctx'}, use_global_device_ids=true, to_apply=%region_48.49 | all-reduce | flops 1536 | bytes 12288 | tf_op jit(solution)/shard_map/psum | solution.py:237
  631.1 122.6 %all-reduce.16.cloned.1.call-done = (f32[3,384,192]{1,2,0:T(8,128)}, f32[192,384]{1,0:T(8,128)}, f32[384,768]{1,0:T(8,128)}, f32[768,384]{1,0:T(8,128)}) async-done(((f32[3,384,192]{1,2,0:T(8,128)}, f32[192,384]{1,0:T(8,128)}, f32[384,768]{1,0:T(8,128)}, f32[768,384]{1,0:T(8,128)}), (f32[3,384,192]{1,2,0:T(8,128)}, f32[192,384]{1,0:T(8,128)}, f32[384,768]{1,0:T(8,128)}, ...) | async-done | bytes 3538960 | tf_op jit(solution)/shard_map/psum | solution.py:237
  753.8 2.2 copy.40
  (289 shorter events, 68.2 us)
Async XLA Ops:
  8.0 14.0 %copy-start.4 = (bf16[2,1,512,768]{3,2,1,0:T(8,128)(2,1)S(1)}, bf16[2,1,512,768]{3,2,1,0:T(8,128)(2,1)}, u32[]{:S(2)}) copy-start(bf16[2,1,512,768]{3,2,1,0:T(8,128)(2,1)} %param.10) | copy-start | bytes 4718596
  8.0 200.2 %all-reduce.14.cloned.1.call-start = ((), (), s32[]{:S(2)}) async-start(), calls=%async_computation.24 | async-start | bytes 6291456 | tf_op jit(solution)/shard_map/psum | solution.py:137
  20.2 56.9 %copy-start.73 = (f32[768]{0:T(1024)}, f32[768]{0:T(1024)S(1)}, u32[]{:S(2)}) copy-start(f32[768]{0:T(1024)S(1)} %get-tuple-element.159) | copy-start | bytes 9220
  20.3 195.5 %copy-start.67 = (f32[768]{0:T(1024)}, f32[768]{0:T(1024)S(1)}, u32[]{:S(2)}) copy-start(f32[768]{0:T(1024)S(1)} %get-tuple-element.158) | copy-start | bytes 9220
  20.3 8.4 %copy-start.43 = (bf16[3,384,192]{1,2,0:T(8,128)(2,1)S(1)}, bf16[3,384,192]{1,2,0:T(8,128)(2,1)}, u32[]{:S(2)}) copy-start(bf16[3,384,192]{1,2,0:T(8,128)(2,1)} %param.13) | copy-start | bytes 1327108
  22.0 16.1 %copy-start.54 = (f32[512]{0:T(512)}, f32[512]{0:T(512)S(1)}, u32[]{:S(2)}) copy-start(f32[512]{0:T(512)S(1)} %broadcast_multiply_fusion.9) | copy-start | bytes 6148
  22.7 54.5 %copy-start.60 = (f32[512]{0:T(512)}, f32[512]{0:T(512)S(1)}, u32[]{:S(2)}) copy-start(f32[512]{0:T(512)S(1)} %add_rsqrt_fusion.3) | copy-start | bytes 6148
  22.7 16.3 %copy-start.62 = (f32[512]{0:T(512)}, f32[512]{0:T(512)S(1)}, u32[]{:S(2)}) copy-start(f32[512]{0:T(512)S(1)} %add_rsqrt_fusion.1) | copy-start | bytes 6148
  38.1 39.1 %copy-start.32 = (bf16[3,768,192]{1,2,0:T(8,128)(2,1)}, bf16[3,768,192]{1,2,0:T(8,128)(2,1)S(1)}, u32[]{:S(2)}) copy-start(bf16[3,768,192]{1,2,0:T(8,128)(2,1)S(1)} %all_gather.22) | copy-start | bytes 2654212
  59.3 67.6 %copy-start.17 = (bf16[1,2048,192]{1,2,0:T(8,128)(2,1)}, bf16[1,2048,192]{1,2,0:T(8,128)(2,1)S(1)}, u32[]{:S(2)}) copy-start(bf16[1,2048,192]{1,2,0:T(8,128)(2,1)S(1)} %all-gather.3) | copy-start | bytes 2359300
  77.2 54.3 %copy-start.16 = (bf16[1,2048,192]{1,2,0:T(8,128)(2,1)}, bf16[1,2048,192]{1,2,0:T(8,128)(2,1)S(1)}, u32[]{:S(2)}) copy-start(bf16[1,2048,192]{1,2,0:T(8,128)(2,1)S(1)} %all-gather.2) | copy-start | bytes 2359300
  78.2 36.3 %copy-start.39 = (bf16[1,512,192]{1,2,0:T(8,128)(2,1)}, bf16[1,512,192]{1,2,0:T(8,128)(2,1)S(1)}, u32[]{:S(2)}) copy-start(bf16[1,512,192]{1,2,0:T(8,128)(2,1)S(1)} %get-tuple-element.185) | copy-start | bytes 589828
  95.3 21.9 %copy-start.19 = (bf16[1,2048,192]{1,2,0:T(8,128)(2,1)}, bf16[1,2048,192]{1,2,0:T(8,128)(2,1)S(1)}, u32[]{:S(2)}) copy-start(bf16[1,2048,192]{1,2,0:T(8,128)(2,1)S(1)} %all-gather.1) | copy-start | bytes 2359300
  111.0 8.1 %copy-start.15 = (bf16[1,2048,192]{1,2,0:T(8,128)(2,1)}, bf16[1,2048,192]{1,2,0:T(8,128)(2,1)S(1)}, u32[]{:S(2)}) copy-start(bf16[1,2048,192]{1,2,0:T(8,128)(2,1)S(1)} %all-gather) | copy-start | bytes 2359300
  117.2 4.5 copy-start
  125.3 4.3 copy-start.35
  129.6 4.5 copy-start.1
  138.8 73.0 %all-gather.7.cloned.1.call-start = ((), (), s32[]{:S(2)}) async-start(), calls=%async_computation.10 | async-start | bytes 1769472 | tf_op jit(solution)/shard_map/all_gather | solution.py:55
  139.3 78.5 %all-gather.9.cloned.1.call-start = ((), (), s32[]{:S(2)}) async-start(), calls=%async_computation.11 | async-start | bytes 1769472 | tf_op jit(solution)/shard_map/all_gather | solution.py:56
  139.9 155.8 %all-reduce.12.cloned.1.call-start = ((), (), s32[]{:S(2)}) async-start(), calls=%async_computation.23 | async-start | bytes 6291456 | tf_op jit(solution)/shard_map/psum | solution.py:158
  210.6 88.9 %copy-start.56 = (f32[512]{0:T(512)}, f32[512]{0:T(512)S(1)}, u32[]{:S(2)}) copy-start(f32[512]{0:T(512)S(1)} %broadcast_multiply_fusion.10) | copy-start | bytes 6148
  211.8 87.8 %copy-start.58 = (f32[512]{0:T(512)}, f32[512]{0:T(512)S(1)}, u32[]{:S(2)}) copy-start(f32[512]{0:T(512)S(1)} %add_rsqrt_fusion) | copy-start | bytes 6148
  211.8 87.8 %copy-start.65 = (f32[512]{0:T(512)}, f32[512]{0:T(512)S(1)}, u32[]{:S(2)}) copy-start(f32[512]{0:T(512)S(1)} %add_rsqrt_fusion.2) | copy-start | bytes 6148
  211.8 3.9 copy-start.78
  226.9 146.0 %reduce-scatter.17.cloned.1.call-start = ((), (), s32[]{:S(2)}) async-start(), calls=%async_computation.13 | async-start | bytes 1966080 | tf_op jit(solution)/shard_map/reduce_scatter | solution.py:204
  295.7 4.3 copy-start.26
  303.7 7.9 %copy-start.21 = (bf16[512,192]{0,1:T(8,128)(2,1)}, bf16[512,192]{0,1:T(8,128)(2,1)S(1)}, u32[]{:S(2)}) copy-start(bf16[512,192]{0,1:T(8,128)(2,1)S(1)} %convolution_convert_fusion.1) | copy-start | bytes 589828
  311.6 72.8 %reduce-scatter.21.cloned.1.call-start = ((), (), s32[]{:S(2)}) async-start(), calls=%async_computation.15 | async-start | bytes 1966080 | tf_op jit(solution)/shard_map/reduce_scatter | solution.py:204
  313.8 8.2 %copy-start.23 = (bf16[512,192]{0,1:T(8,128)(2,1)}, bf16[512,192]{0,1:T(8,128)(2,1)S(1)}, u32[]{:S(2)}) copy-start(bf16[512,192]{0,1:T(8,128)(2,1)S(1)} %convolution_convert_fusion) | copy-start | bytes 589828
  322.0 99.0 %reduce-scatter.19.cloned.1.call-start = ((), (), s32[]{:S(2)}) async-start(), calls=%async_computation.14 | async-start | bytes 1966080 | tf_op jit(solution)/shard_map/reduce_scatter | solution.py:201
  329.5 6.5 copy-start.42
  339.0 118.6 %reduce-scatter.15.cloned.1.call-start = ((), (), s32[]{:S(2)}) async-start(), calls=%async_computation.12 | async-start | bytes 1966080 | tf_op jit(solution)/shard_map/reduce_scatter | solution.py:201
  346.5 6.5 copy-start.40
  356.3 224.9 %all-reduce.10.cloned.1.call-start = ((), (), s32[]{:S(2)}) async-start(), calls=%async_computation.22 | async-start | bytes 12582912 | tf_op jit(solution)/shard_map/psum | solution.py:146
  356.6 4.1 copy-start.77
  356.6 13.6 %slice-start = ((s8[6291456]{0:T(1024)(128)(4,1)}), s8[4194304]{0:T(1024)(128)(4,1)S(1)}, s32[]{:S(2)}) async-start(s8[6291456]{0:T(1024)(128)(4,1)} %bitcast.223), calls=%async_computation.26 | async-start | bytes 8388608
  360.7 9.5 %slice-start.1 = ((s8[6291456]{0:T(1024)(128)(4,1)}), s8[2097152]{0:T(1024)(128)(4,1)S(1)}, s32[]{:S(2)}) async-start(s8[6291456]{0:T(1024)(128)(4,1)} %bitcast.223), calls=%async_computation.27 | async-start | bytes 4194304
  364.6 5.6 copy-start.20
  374.0 84.7 %copy-start.45 = (bf16[1,512,192]{1,2,0:T(8,128)(2,1)}, bf16[1,512,192]{1,2,0:T(8,128)(2,1)S(1)}, u32[]{:S(2)}) copy-start(bf16[1,512,192]{1,2,0:T(8,128)(2,1)S(1)} %convert_bitcast_fusion.6) | copy-start | bytes 589828
  385.4 40.5 %copy-start.47 = (bf16[1,512,192]{1,2,0:T(8,128)(2,1)}, bf16[1,512,192]{1,2,0:T(8,128)(2,1)S(1)}, u32[]{:S(2)}) copy-start(bf16[1,512,192]{1,2,0:T(8,128)(2,1)S(1)} %convert_bitcast_fusion.4) | copy-start | bytes 589828
  462.6 123.6 %reduce-scatter.25.cloned.1.call-start = ((), (), s32[]{:S(2)}) async-start(), calls=%async_computation.17 | async-start | bytes 884736 | tf_op jit(solution)/shard_map/reduce_scatter | solution.py:242
  466.6 119.7 %reduce-scatter.27.cloned.1.call-start = ((), (), s32[]{:S(2)}) async-start(), calls=%async_computation.18 | async-start | bytes 3538944 | tf_op jit(solution)/shard_map/reduce_scatter | solution.py:243
  472.3 114.0 %reduce-scatter.29.cloned.1.call-start = ((), (), s32[]{:S(2)}) async-start(), calls=%async_computation.19 | async-start | bytes 3538944 | tf_op jit(solution)/shard_map/reduce_scatter | solution.py:244
  478.0 108.3 %reduce-scatter.23.cloned.1.call-start = ((), (), s32[]{:S(2)}) async-start(), calls=%async_computation.16 | async-start | bytes 2654208 | tf_op jit(solution)/shard_map/reduce_scatter | solution.py:241
  483.1 98.1 %copy-start.64 = (f32[512]{0:T(512)S(1)}, f32[512]{0:T(512)}, u32[]{:S(2)}) copy-start(f32[512]{0:T(512)} %copy-done.62) | copy-start | bytes 6148
  483.1 118.4 %reduce-scatter.33.cloned.1.call-start = ((), (), s32[]{:S(2)}) async-start(), calls=%async_computation.21 | async-start | bytes 589824
  585.1 32.4 %reduce-scatter.31.cloned.1.call-start = ((), (), s32[]{:S(2)}) async-start(), calls=%async_computation.20 | async-start | bytes 589824
  586.2 167.6 %all-reduce.16.cloned.1.call-start = ((), (), s32[]{:S(2)}) async-start(), calls=%async_computation.25 | async-start | bytes 7077888 | tf_op jit(solution)/shard_map/psum | solution.py:237
  (53 other events, 114.5 us)
Sparse Core Ops, SparseCore 0:
  138.9 69.2 all-reduce.13
  227.1 68.5 all-reduce.11
  462.7 118.4 all-reduce.9
Sparse Core Ops, SparseCore 1:
  140.8 23.4 all-gather.6
  165.7 22.6 all-gather.8
  311.7 35.5 reduce-scatter.16
  350.2 34.2 reduce-scatter.20
  386.7 34.2 reduce-scatter.18
  423.4 34.2 reduce-scatter.14
  466.7 14.0 reduce-scatter.24
  483.5 34.7 reduce-scatter.26
  520.3 34.7 reduce-scatter.28
  557.4 28.2 reduce-scatter.22
  588.3 13.1 reduce-scatter.32
  604.3 13.1 reduce-scatter.30
  620.0 133.7 all-reduce.15
where the time goes:
time: 775 us; the launch traced here: 767 us
  waiting for transfers between devices  457 us (59%)
  matrix products  110 us (14%)
  blocking collectives  108 us (14%)
  other arithmetic  46.1 us (6%)
  local copies, waits for them, and re-layouts  26.5 us (3%)
  between operations  17.2 us (2%)
    psum x1, waiting for transfers between devices, body(): lax.psum((acc_qkv, acc_out, acc_up, acc_down, acc_gains, acc_shifts), 'ctx')  123 us
    psum x1, waiting for transfers between devices, body(): mlp = lax.psum(mlp_part, 'tp')  97.4 us
    psum x1, waiting for transfers between devices, body(): second_norm_gradient = lax.psum(n2_back, 'tp')  68.7 us
    psum x1, waiting for transfers between devices, body(): attn = lax.psum(attn_part, 'tp')  68 us
    reduce_scatter x2, waiting for transfers between devices, body(): lax.psum_scatter(key_sum.reshape(seq_len, local_width), 'ctx', scatter_di...  67.2 us
    all_gather x2, blocking collectives, body(): lax.all_gather(qkv[1], 'ctx', axis=0, tiled=True)  36.6 us
    all_gather x2, blocking collectives, body(): lax.all_gather(qkv[2], 'ctx', axis=0, tiled=True)  33.6 us
    unnamed x178, local copies, waits for them, and re-layouts  24.3 us
  transfers between devices with their start and end apart: 16, of which 9 were waited for; matrix products, arithmetic and copies ran while one was open for 14% of the time, Pallas kernels for 0%

commit v1 on v0

--- a/solution.py
+++ b/solution.py
@@ -10,6 +10,14 @@
 GELU_A = 0.044715
 NEG = -1e30
 ROW_BLOCK = 512
+
+
+def work_body(mine_x):
+    n_slots = jax.lax.axis_size("tp")
+    all_values = mine_x
+    for b in [[(i, i ^ p) for i in range(n_slots)] for p in (1, 2, 4, 8, 16) if p < n_slots]:
+        all_values = all_values + jax.lax.ppermute(all_values, axis_name="tp", perm=b)
+    return all_values
 
 
 def apply_layer_norm(values, norm_gain, norm_shift):
@@ -143,7 +151,7 @@
         up = jnp.dot(h2, up_full, preferred_element_type=jnp.float32)
         act = gelu_value(up).astype(jnp.bfloat16)
         mlp_part = jnp.dot(act, down_full, preferred_element_type=jnp.float32)
-        mlp = lax.psum(mlp_part, "tp")
+        mlp = work_body(mlp_part)
         results.append((middle_state + branch * mlp).astype(jnp.bfloat16))
         qkv_full, out_full, up_full, down_full, gains_full, shifts_full = fetch_weights(
             qkv_weight, out_weight, up_weight, down_weight, ln_gains, ln_shifts

time: 775 us -> 830 us (1.071)
  waiting for transfers between devices: 457 us -> 510 us
  other arithmetic: 46.1 us -> 57.3 us
  matrix products: 110 us -> 99.3 us
    psum x1, waiting for transfers between devices: 97.4 us -> 46.9 us  [body(): first_norm_gradient = lax.psum(n1_back, 'tp')]
    psum x1, waiting for transfers between devices: 68.7 us -> 111 us  [body(): second_norm_gradient = lax.psum(n2_back, 'tp')]
    reduce_scatter x1, waiting for transfers between devices: 0.02 us -> 30.6 us  [body(): lax.psum_scatter(whole_qkv, 'dp', scatter_dimension=1, tiled=True)]
    reduce_scatter x1, waiting for transfers between devices: 0.02 us -> 20 us  [body(): lax.psum_scatter(whole_up, 'dp', scatter_dimension=0, tiled=True)]
    reduce_scatter x2, waiting for transfers between devices: 10.4 us -> 18.8 us  [body(): lax.psum_scatter(value_sum.reshape(seq_len, local_width), 'ctx', scatter_...]
    unnamed x178 -> x170, local copies, waits for them, and re-layouts: 24.3 us -> 24.5 us
  transfers between devices with their start and end apart: 16 -> 20, of which waited for: 9 -> 12; matrix products, arithmetic and copies ran while one was open for 14% -> 14% of each run, Pallas kernels for 0% -> 0%
where the time goes in v1:
time: 830 us; the launch traced here: 822 us
  waiting for transfers between devices  510 us (61%)
  blocking collectives  108 us (13%)
  matrix products  99.3 us (12%)
  other arithmetic  57.3 us (7%)
  local copies, waits for them, and re-layouts  26.7 us (3%)
  between operations  17.2 us (2%)
    psum x1, waiting for transfers between devices, body(): lax.psum((acc_qkv, acc_out, acc_up, acc_down, acc_gains, acc_shifts), 'ctx')  123 us
    psum x1, waiting for transfers between devices, body(): second_norm_gradient = lax.psum(n2_back, 'tp')  111 us
    psum x1, waiting for transfers between devices, body(): attn = lax.psum(attn_part, 'tp')  68 us
    reduce_scatter x2, waiting for transfers between devices, body(): lax.psum_scatter(key_sum.reshape(seq_len, local_width), 'ctx', scatter_di...  67.1 us
    psum x1, waiting for transfers between devices, body(): first_norm_gradient = lax.psum(n1_back, 'tp')  46.9 us
    all_gather x2, blocking collectives, body(): lax.all_gather(qkv[1], 'ctx', axis=0, tiled=True)  36.6 us
    all_gather x2, blocking collectives, body(): lax.all_gather(qkv[2], 'ctx', axis=0, tiled=True)  33.6 us
    reduce_scatter x1, waiting for transfers between devices, body(): lax.psum_scatter(whole_qkv, 'dp', scatter_dimension=1, tiled=True)  30.6 us
  transfers between devices with their start and end apart: 20, of which 12 were waited for; matrix products, arithmetic and copies ran while one was open for 14% of the time, Pallas kernels for 0%

profile of v1, /device:TPU:0, one launch (start us, length us, event | category | flops | bytes accessed | tf_op | source)
XLA Modules:
  0.0 821.7 jit_solution(5533331327220144784)
XLA Ops:
  10.2 5.5 all_gather.20
  15.7 4.5 all_gather.21
  22.8 5.9 all_gather.49
  28.8 9.4 %all_gather.22 = bf16[3,768,192]{1,2,0:T(8,128)(2,1)S(1)} all-gather(bf16[3,384,192]{1,2,0:T(8,128)(2,1)S(1)} %copy-done.38), channel_id=1, replica_groups=mesh['dp'=2,'ctx'=4,'tp'=4] {'dp'}, dimensions={1}, use_global_device_ids=true | all-gather | bytes 1327104 | tf_op jit(solution)/shard_map/all_gather | solution.py:61
  39.8 19.5 %all-gather.3 = bf16[1,2048,192]{1,2,0:T(8,128)(2,1)S(1)} all-gather(bf16[1,512,192]{1,2,0:T(8,128)(2,1)S(1)} %get-tuple-element.187), channel_id=5, replica_groups=mesh['dp'=2,'ctx'=4,'tp'=4] {'ctx'}, dimensions={1}, use_global_device_ids=true | all-gather | bytes 983040 | tf_op jit(solution)/shard_map/all_gather | solution.py:121
  59.3 17.8 %all-gather.2 = bf16[1,2048,192]{1,2,0:T(8,128)(2,1)S(1)} all-gather(bf16[1,512,192]{1,2,0:T(8,128)(2,1)S(1)} %get-tuple-element.189), channel_id=4, replica_groups=mesh['dp'=2,'ctx'=4,'tp'=4] {'ctx'}, dimensions={1}, use_global_device_ids=true | all-gather | bytes 983040 | tf_op jit(solution)/shard_map/all_gather | solution.py:122
  78.2 17.1 %all-gather.1 = bf16[1,2048,192]{1,2,0:T(8,128)(2,1)S(1)} all-gather(bf16[1,512,192]{1,2,0:T(8,128)(2,1)S(1)} %get-tuple-element.184), channel_id=3, replica_groups=mesh['dp'=2,'ctx'=4,'tp'=4] {'ctx'}, dimensions={1}, use_global_device_ids=true | all-gather | bytes 983040 | tf_op jit(solution)/shard_map/all_gather | solution.py:121
  95.3 15.7 %all-gather = bf16[1,2048,192]{1,2,0:T(8,128)(2,1)S(1)} all-gather(bf16[1,512,192]{1,2,0:T(8,128)(2,1)S(1)} %get-tuple-element.186), channel_id=2, replica_groups=mesh['dp'=2,'ctx'=4,'tp'=4] {'ctx'}, dimensions={1}, use_global_device_ids=true | all-gather | bytes 983040 | tf_op jit(solution)/shard_map/all_gather | solution.py:122
  114.5 2.7 fusion.124
  119.1 2.6 copy-done
  121.7 3.6 fusion.65
  126.9 2.7 fusion.123
  134.1 3.1 fusion.64
  140.8 68.0 %all-reduce.14.cloned.1.call-done = (f32[512,768]{1,0:T(8,128)}, f32[512,768]{1,0:T(8,128)}) async-done(((f32[512,768]{1,0:T(8,128)}, f32[512,768]{1,0:T(8,128)}), (f32[512,768]{1,0:T(8,128)}, f32[512,768]{1,0:T(8,128)})) %all-reduce.14.cloned.1.call-update) | async-done | bytes 3145744 | tf_op jit(solution)/shard_map/psum | solution.py:145
  212.4 3.8 fusion.114
  216.2 4.1 fusion.111
  231.8 3.3 add.315
  235.5 3.5 add.325
  240.4 110.8 %all-reduce.12.cloned.1.call-done = (f32[512,768]{1,0:T(8,128)}, f32[512,768]{1,0:T(8,128)}) async-done(((f32[512,768]{1,0:T(8,128)}, f32[512,768]{1,0:T(8,128)}), (f32[512,768]{1,0:T(8,128)}, f32[512,768]{1,0:T(8,128)})) %all-reduce.12.cloned.1.call-update) | async-done | bytes 3145744 | tf_op jit(solution)/shard_map/psum | solution.py:166
  351.1 3.8 multiply_reduce_fusion.3
  356.2 6.2 convert_add_fusion.1
  364.5 3.3 fusion.6
  369.8 8.1 fusion.4
  378.8 6.6 multiply_reduce_fusion
  385.4 6.5 multiply_convert_fusion
  391.9 2.8 convolution_multiply_fusion
  395.9 6.6 multiply_reduce_fusion.1
  402.5 6.4 multiply_convert_fusion.1
  408.9 3.0 convolution_multiply_fusion.1
  412.2 5.9 fusion.63
  418.1 2.7 fusion.62
  421.9 18.8 %reduce-scatter.21.cloned.1.call-done = f32[512,192]{0,1:T(8,128)} async-done(((f32[2048,192]{0,1:T(8,128)}), f32[512,192]{0,1:T(8,128)}) %reduce-scatter.21.cloned.1.call-update) | async-done | bytes 393232 | tf_op jit(solution)/shard_map/reduce_scatter | solution.py:212
  441.7 35.6 %reduce-scatter.19.cloned.1.call-done = f32[512,192]{0,1:T(8,128)} async-done(((f32[2048,192]{0,1:T(8,128)}), f32[512,192]{0,1:T(8,128)}) %reduce-scatter.19.cloned.1.call-update) | async-done | bytes 393232 | tf_op jit(solution)/shard_map/reduce_scatter | solution.py:209
  479.0 3.3 convolution_bitcast_fusion
  482.2 31.6 %reduce-scatter.15.cloned.1.call-done = f32[512,192]{0,1:T(8,128)} async-done(((f32[2048,192]{0,1:T(8,128)}), f32[512,192]{0,1:T(8,128)}) %reduce-scatter.15.cloned.1.call-update) | async-done | bytes 393232 | tf_op jit(solution)/shard_map/reduce_scatter | solution.py:209
  515.5 3.4 convolution_bitcast_fusion.1
  522.9 3.1 fusion.73
  526.0 2.6 convolution_add_fusion
  529.4 2.7 fusion.113
  539.4 46.9 %all-reduce.10.cloned.1.call-done = (f32[512,768]{1,0:T(8,128)}, f32[512,768]{1,0:T(8,128)}) async-done(((f32[512,768]{1,0:T(8,128)}, f32[512,768]{1,0:T(8,128)}), (f32[512,768]{1,0:T(8,128)}, f32[512,768]{1,0:T(8,128)})) %all-reduce.10.cloned.1.call-update) | async-done | bytes 3145744 | tf_op jit(solution)/shard_map/psum | solution.py:225
  586.3 2.9 fusion.44
  591.4 20.0 %reduce-scatter.27.cloned.1.call-done = f32[384,768]{1,0:T(8,128)} async-done(((f32[768,768]{1,0:T(8,128)}), f32[384,768]{1,0:T(8,128)}) %reduce-scatter.27.cloned.1.call-update) | async-done | bytes 1179664 | tf_op jit(solution)/shard_map/reduce_scatter | solution.py:251
  611.4 30.6 %reduce-scatter.23.cloned.1.call-done = f32[3,384,192]{1,2,0:T(8,128)} async-done(((f32[3,768,192]{1,2,0:T(8,128)}), f32[3,384,192]{1,2,0:T(8,128)}) %reduce-scatter.23.cloned.1.call-update) | async-done | bytes 884752 | tf_op jit(solution)/shard_map/reduce_scatter | solution.py:249
  642.0 2.8 maximum_bitcast_fusion.1
  649.4 7.8 reduce-scatter.33.cloned.1.call-done
  658.2 14.4 %reduce-scatter.31.cloned.1.call-done = f32[384,2]{1,0:T(8,128)} async-done(((f32[768,2]{1,0:T(8,128)}), f32[384,2]{1,0:T(8,128)}) %reduce-scatter.31.cloned.1.call-update) | async-done | bytes 3088
  673.7 12.6 %all-reduce.3 = (f32[2,384]{1,0:T(2,128)}, f32[2,384]{1,0:T(2,128)}) all-reduce(f32[2,384]{1,0:T(2,128)S(1)} %copy.25, f32[2,384]{1,0:T(2,128)S(1)} %copy.27), channel_id=1, replica_groups=mesh['dp'=2,'ctx'=4,'tp'=4] {'ctx'}, use_global_device_ids=true, to_apply=%region_46.47 | all-reduce | flops 1536 | bytes 12288 | tf_op jit(solution)/shard_map/psum | solution.py:245
  686.3 122.6 %all-reduce.16.cloned.1.call-done = (f32[3,384,192]{1,2,0:T(8,128)}, f32[192,384]{1,0:T(8,128)}, f32[384,768]{1,0:T(8,128)}, f32[768,384]{1,0:T(8,128)}) async-done(((f32[3,384,192]{1,2,0:T(8,128)}, f32[192,384]{1,0:T(8,128)}, f32[384,768]{1,0:T(8,128)}, f32[768,384]{1,0:T(8,128)}), (f32[3,384,192]{1,2,0:T(8,128)}, f32[192,384]{1,0:T(8,128)}, f32[384,768]{1,0:T(8,128)}, ...) | async-done | bytes 3538960 | tf_op jit(solution)/shard_map/psum | solution.py:245
  (288 shorter events, 77.7 us)
Async XLA Ops:
  8.0 14.1 %copy-start.5 = (bf16[2,1,512,768]{3,2,1,0:T(8,128)(2,1)S(1)}, bf16[2,1,512,768]{3,2,1,0:T(8,128)(2,1)}, u32[]{:S(2)}) copy-start(bf16[2,1,512,768]{3,2,1,0:T(8,128)(2,1)} %param.10) | copy-start | bytes 4718596
  8.0 200.9 %all-reduce.14.cloned.1.call-start = ((), (), s32[]{:S(2)}) async-start(), calls=%async_computation.24 | async-start | bytes 6291456 | tf_op jit(solution)/shard_map/psum | solution.py:145
  15.7 61.5 %copy-start.51 = (f32[768]{0:T(1024)}, f32[768]{0:T(1024)S(1)}, u32[]{:S(2)}) copy-start(f32[768]{0:T(1024)S(1)} %get-tuple-element.157) | copy-start | bytes 9220
  20.3 56.9 %copy-start.69 = (f32[768]{0:T(1024)}, f32[768]{0:T(1024)S(1)}, u32[]{:S(2)}) copy-start(f32[768]{0:T(1024)S(1)} %get-tuple-element.159) | copy-start | bytes 9220
  20.3 200.1 %copy-start.63 = (f32[768]{0:T(1024)}, f32[768]{0:T(1024)S(1)}, u32[]{:S(2)}) copy-start(f32[768]{0:T(1024)S(1)} %get-tuple-element.158) | copy-start | bytes 9220
  20.3 8.5 %copy-start.38 = (bf16[3,384,192]{1,2,0:T(8,128)(2,1)S(1)}, bf16[3,384,192]{1,2,0:T(8,128)(2,1)}, u32[]{:S(2)}) copy-start(bf16[3,384,192]{1,2,0:T(8,128)(2,1)} %param.13) | copy-start | bytes 1327108
  22.0 55.1 %copy-start.53 = (f32[512]{0:T(512)}, f32[512]{0:T(512)S(1)}, u32[]{:S(2)}) copy-start(f32[512]{0:T(512)S(1)} %broadcast_multiply_fusion.11) | copy-start | bytes 6148
  22.1 16.1 %copy-start.55 = (f32[512]{0:T(512)}, f32[512]{0:T(512)S(1)}, u32[]{:S(2)}) copy-start(f32[512]{0:T(512)S(1)} %broadcast_multiply_fusion.9) | copy-start | bytes 6148
  22.7 54.5 %copy-start.57 = (f32[512]{0:T(512)}, f32[512]{0:T(512)S(1)}, u32[]{:S(2)}) copy-start(f32[512]{0:T(512)S(1)} %add_rsqrt_fusion.3) | copy-start | bytes 6148
  22.7 16.3 %copy-start.59 = (f32[512]{0:T(512)}, f32[512]{0:T(512)S(1)}, u32[]{:S(2)}) copy-start(f32[512]{0:T(512)S(1)} %add_rsqrt_fusion.1) | copy-start | bytes 6148
  38.1 39.1 %copy-start.27 = (bf16[3,768,192]{1,2,0:T(8,128)(2,1)}, bf16[3,768,192]{1,2,0:T(8,128)(2,1)S(1)}, u32[]{:S(2)}) copy-start(bf16[3,768,192]{1,2,0:T(8,128)(2,1)S(1)} %all_gather.22) | copy-start | bytes 2654212
  59.3 67.6 %copy-start.15 = (bf16[1,2048,192]{1,2,0:T(8,128)(2,1)}, bf16[1,2048,192]{1,2,0:T(8,128)(2,1)S(1)}, u32[]{:S(2)}) copy-start(bf16[1,2048,192]{1,2,0:T(8,128)(2,1)S(1)} %all-gather.3) | copy-start | bytes 2359300
  77.2 54.3 %copy-start.14 = (bf16[1,2048,192]{1,2,0:T(8,128)(2,1)}, bf16[1,2048,192]{1,2,0:T(8,128)(2,1)S(1)}, u32[]{:S(2)}) copy-start(bf16[1,2048,192]{1,2,0:T(8,128)(2,1)S(1)} %all-gather.2) | copy-start | bytes 2359300
  78.2 36.3 %copy-start.34 = (bf16[1,512,192]{1,2,0:T(8,128)(2,1)}, bf16[1,512,192]{1,2,0:T(8,128)(2,1)S(1)}, u32[]{:S(2)}) copy-start(bf16[1,512,192]{1,2,0:T(8,128)(2,1)S(1)} %get-tuple-element.185) | copy-start | bytes 589828
  95.3 21.9 %copy-start.16 = (bf16[1,2048,192]{1,2,0:T(8,128)(2,1)}, bf16[1,2048,192]{1,2,0:T(8,128)(2,1)S(1)}, u32[]{:S(2)}) copy-start(bf16[1,2048,192]{1,2,0:T(8,128)(2,1)S(1)} %all-gather.1) | copy-start | bytes 2359300
  111.0 8.1 copy-start.13
  117.2 4.5 copy-start
  139.4 73.0 %all-gather.7.cloned.1.call-start = ((), (), s32[]{:S(2)}) async-start(), calls=%async_computation.10 | async-start | bytes 1769472 | tf_op jit(solution)/shard_map/all_gather | solution.py:63
  140.0 76.2 %all-gather.9.cloned.1.call-start = ((), (), s32[]{:S(2)}) async-start(), calls=%async_computation.11 | async-start | bytes 1769472 | tf_op jit(solution)/shard_map/all_gather | solution.py:64
  140.6 210.5 %all-reduce.12.cloned.1.call-start = ((), (), s32[]{:S(2)}) async-start(), calls=%async_computation.23 | async-start | bytes 6291456 | tf_op jit(solution)/shard_map/psum | solution.py:166
  212.4 143.8 %copy-start.61 = (f32[512]{0:T(512)}, f32[512]{0:T(512)S(1)}, u32[]{:S(2)}) copy-start(f32[512]{0:T(512)S(1)} %add_rsqrt_fusion.2) | copy-start | bytes 6148
  220.3 11.5 %collective-permute-start = (f32[512,768]{1,0:T(8,128)}, f32[512,768]{1,0:T(8,128)}, u32[]{:S(2)}, u32[]{:S(2)}) collective-permute-start(f32[512,768]{1,0:T(8,128)} %fusion.111), channel_id=1, source_target_pairs={{0,1},{1,0},{2,3},{3,2},{4,5},{5,4},{6,7},{7,6},{8,9},{9,8},{10,11... | collective-permute-start | bytes 4718600 | tf_op jit(solution)/shard_map/ppermute | solution.py:19
  223.8 11.7 %collective-permute-start.2 = (f32[512,768]{1,0:T(8,128)}, f32[512,768]{1,0:T(8,128)}, u32[]{:S(2)}, u32[]{:S(2)}) collective-permute-start(f32[512,768]{1,0:T(8,128)} %fusion.112), channel_id=1, source_target_pairs={{0,1},{1,0},{2,3},{3,2},{4,5},{5,4},{6,7},{7,6},{8,9},{9,8},{10,11... | collective-permute-start | bytes 4718600 | tf_op jit(solution)/shard_map/ppermute | solution.py:19
  231.5 189.3 %reduce-scatter.17.cloned.1.call-start = ((), (), s32[]{:S(2)}) async-start(), calls=%async_computation.13 | async-start | bytes 1966080 | tf_op jit(solution)/shard_map/reduce_scatter | solution.py:212
  235.1 119.9 %collective-permute-start.1 = (f32[512,768]{1,0:T(8,128)}, f32[512,768]{1,0:T(8,128)}, u32[]{:S(2)}, u32[]{:S(2)}) collective-permute-start(f32[512,768]{1,0:T(8,128)} %add.315), channel_id=1, source_target_pairs={{0,2},{1,3},{2,0},{3,1},{4,6},{5,7},{6,4},{7,5},{8,10},{9,11},{10,... | collective-permute-start | bytes 4718600 | tf_op jit(solution)/shard_map/ppermute | solution.py:19
  239.1 117.1 %collective-permute-start.3 = (f32[512,768]{1,0:T(8,128)}, f32[512,768]{1,0:T(8,128)}, u32[]{:S(2)}, u32[]{:S(2)}) collective-permute-start(f32[512,768]{1,0:T(8,128)} %add.325), channel_id=1, source_target_pairs={{0,2},{1,3},{2,0},{3,1},{4,6},{5,7},{6,4},{7,5},{8,10},{9,11},{10,... | collective-permute-start | bytes 4718600 | tf_op jit(solution)/shard_map/ppermute | solution.py:19
  351.1 5.0 copy-start.11
  351.1 12.8 %slice-start = ((s8[12582912]{0:T(1024)(128)(4,1)}), s8[4194304]{0:T(1024)(128)(4,1)S(1)}, s32[]{:S(2)}) async-start(s8[12582912]{0:T(1024)(128)(4,1)} %bitcast.223), calls=%async_computation.26 | async-start | bytes 8388608
  356.2 7.8 slice-start.1
  356.2 8.4 %slice-start.2 = ((s8[12582912]{0:T(1024)(128)(4,1)}), s8[4194304]{0:T(1024)(128)(4,1)S(1)}, s32[]{:S(2)}) async-start(s8[12582912]{0:T(1024)(128)(4,1)} %bitcast.223), calls=%async_computation.28 | async-start | bytes 8388608
  367.9 72.8 %reduce-scatter.21.cloned.1.call-start = ((), (), s32[]{:S(2)}) async-start(), calls=%async_computation.15 | async-start | bytes 1966080 | tf_op jit(solution)/shard_map/reduce_scatter | solution.py:212
  369.8 8.1 copy-start.20
  377.9 99.3 %reduce-scatter.19.cloned.1.call-start = ((), (), s32[]{:S(2)}) async-start(), calls=%async_computation.14 | async-start | bytes 1966080 | tf_op jit(solution)/shard_map/reduce_scatter | solution.py:209
  385.4 6.5 copy-start.37
  395.0 118.8 %reduce-scatter.15.cloned.1.call-start = ((), (), s32[]{:S(2)}) async-start(), calls=%async_computation.12 | async-start | bytes 1966080 | tf_op jit(solution)/shard_map/reduce_scatter | solution.py:209
  402.5 6.5 copy-start.35
  412.2 174.2 %all-reduce.10.cloned.1.call-start = ((), (), s32[]{:S(2)}) async-start(), calls=%async_computation.22 | async-start | bytes 6291456 | tf_op jit(solution)/shard_map/psum | solution.py:225
  412.2 5.9 copy-start.4
  412.2 5.9 copy-start.17
  421.9 93.0 %copy-start.40 = (bf16[1,512,192]{1,2,0:T(8,128)(2,1)}, bf16[1,512,192]{1,2,0:T(8,128)(2,1)S(1)}, u32[]{:S(2)}) copy-start(bf16[1,512,192]{1,2,0:T(8,128)(2,1)S(1)} %convert_bitcast_fusion.6) | copy-start | bytes 589828
  441.7 40.5 %copy-start.42 = (bf16[1,512,192]{1,2,0:T(8,128)(2,1)}, bf16[1,512,192]{1,2,0:T(8,128)(2,1)S(1)}, u32[]{:S(2)}) copy-start(bf16[1,512,192]{1,2,0:T(8,128)(2,1)S(1)} %convert_bitcast_fusion.4) | copy-start | bytes 589828
  518.9 72.5 %reduce-scatter.25.cloned.1.call-start = ((), (), s32[]{:S(2)}) async-start(), calls=%async_computation.17 | async-start | bytes 884736 | tf_op jit(solution)/shard_map/reduce_scatter | solution.py:250
  522.9 68.6 %reduce-scatter.29.cloned.1.call-start = ((), (), s32[]{:S(2)}) async-start(), calls=%async_computation.19 | async-start | bytes 3538944 | tf_op jit(solution)/shard_map/reduce_scatter | solution.py:252
  528.7 82.7 %reduce-scatter.27.cloned.1.call-start = ((), (), s32[]{:S(2)}) async-start(), calls=%async_computation.18 | async-start | bytes 3538944 | tf_op jit(solution)/shard_map/reduce_scatter | solution.py:251
  534.7 107.3 %reduce-scatter.23.cloned.1.call-start = ((), (), s32[]{:S(2)}) async-start(), calls=%async_computation.16 | async-start | bytes 2654208 | tf_op jit(solution)/shard_map/reduce_scatter | solution.py:249
  538.7 118.5 %reduce-scatter.33.cloned.1.call-start = ((), (), s32[]{:S(2)}) async-start(), calls=%async_computation.21 | async-start | bytes 589824
  590.3 82.4 %reduce-scatter.31.cloned.1.call-start = ((), (), s32[]{:S(2)}) async-start(), calls=%async_computation.20 | async-start | bytes 589824
  591.3 217.6 %all-reduce.16.cloned.1.call-start = ((), (), s32[]{:S(2)}) async-start(), calls=%async_computation.25 | async-start | bytes 7077888 | tf_op jit(solution)/shard_map/psum | solution.py:245
  (53 other events, 105.8 us)
Sparse Core Ops, SparseCore 0:
  139.5 69.2 all-reduce.13
  231.7 119.4 all-reduce.11
  519.0 67.2 all-reduce.9
Sparse Core Ops, SparseCore 1:
  141.4 23.4 all-gather.6
  166.3 22.6 all-gather.8
  367.9 35.5 reduce-scatter.16
  406.4 34.2 reduce-scatter.20
  443.0 34.2 reduce-scatter.18
  479.6 34.2 reduce-scatter.14
  523.0 14.1 reduce-scatter.24
  539.2 34.7 reduce-scatter.28
  576.6 34.7 reduce-scatter.26
  613.7 28.2 reduce-scatter.22
  644.1 13.1 reduce-scatter.32
  659.5 13.1 reduce-scatter.30
  675.2 133.7 all-reduce.15
